TPU v7x, 32 devices: a whole 2x2x4 slice. The times are simulated.
32 devices in a mesh: ctx: 8 (over y, x, core), shard: 4 (over z).
Axes of the slice: x: 2, y: 2, z: 4, core: 2. Of those that a mesh axis runs over, the one named last changes fastest.
Arguments:
- hidden_in: bfloat16 [8, 1024, 768], P('shard', 'ctx'), may hold values from -6 to 6
- block_of: int32 [16], replicated, may hold values from 0 to 15, each once
- lengths: int32 [8], replicated, may hold values from 256 to 1024, as said below
- attn_latent: float32 [4, 768, 768], P(None, 'shard'), may hold values from -1.25 to 1.25
- ffn_in_latent: float32 [768, 3072], P('shard'), may hold values from -1.25 to 1.25
- ffn_out_latent: float32 [3072, 768], P('shard'), may hold values from -1.25 to 1.25
- student_vec: float32 [12, 768], replicated
- teacher_attn: bfloat16 [4, 768, 768], P(None, 'shard'), may hold values from -0.3125 to 0.3125
- teacher_ffn_in: bfloat16 [768, 3072], P('shard'), may hold values from -0.21875 to 0.21875
- teacher_ffn_out: bfloat16 [3072, 768], P('shard'), may hold values from -0.109375 to 0.109375
- teacher_vec: float32 [12, 768], replicated
Outputs:
- output: bfloat16 [8, 1024, 768], P('shard', 'ctx')
- statistics: float32 [4], replicated
- grad_hidden: float32 [8, 1024, 768], P('shard', 'ctx')
- grad_attn_latent: float32 [4, 768, 768], P(None, 'shard')
- grad_ffn_in_latent: float32 [768, 3072], P('shard')
- grad_ffn_out_latent: float32 [3072, 768], P('shard')
- grad_student_vec: float32 [11, 768], replicated
- grad_query_bias: float32 [768], replicated
Inputs may be any that keep to these rules, and one draw needn't show every extreme that they name: `block_of`: every block of 64 places of a sequence is named once; entry q holds the block that lies at layout places q * 64 to (q + 1) * 64 - 1, the same for every sequence. `lengths`: A token is valid where its place is below its sequence's length; some sequence has length 1024.
All inputs are finite; a program needn't handle non-finite values.
Results may differ from a plain program's by a relative error of at most 0.0097.
Values may be sent and summed in bfloat16 or wider, within the bound.
No kernel may reach another device: no remote copies, remote signals or barrier semaphores. Data moves between devices by JAX's collectives and lax.ppermute only.
A program may use at most 320 MiB of HBM per device.

v0:
```python
import jax
import jax.numpy as jnp
from jax import lax
from jax.sharding import PartitionSpec as P

D = 768
HEADS = 12
HEAD_DIM = 64
FF = 3072
BLK = 64
norm_eps = 1e-05
attn_gains = (2.0, 2.0, 1.0, 4.0)
heads_block = 4
masked_score = -1e30


def layer_norm(values, gain, shift):
    middle = jnp.mean(values, axis=-1, keepdims=True)
    centred = values - middle
    spread = jnp.mean(centred * centred, axis=-1, keepdims=True)
    return centred * lax.rsqrt(spread + norm_eps) * gain + shift


def gelu_exact(values):
    return jax.nn.gelu(values, approximate=False)


def matmul(left_side, right_side):
    return jnp.dot(left_side, right_side, preferred_element_type=jnp.float32)


def left_product(left_side, right_side):
    return lax.dot_general(
        left_side, right_side, (((0,), (0,)), ((), ())), preferred_element_type=jnp.float32
    )


def right_product(left_side, right_side):
    return lax.dot_general(
        left_side, right_side, (((1,), (1,)), ((), ())), preferred_element_type=jnp.float32
    )


def binarize(latent, column_sum, gain, fan_in):
    return (gain * (column_sum / fan_in) * jnp.sign(latent) * fan_in ** (-0.5)).astype(jnp.bfloat16)


def positions_of(block_of):
    return (block_of[:, None] * BLK + jnp.arange(BLK, dtype=jnp.int32)[None, :]).reshape(
        block_of.shape[0] * BLK
    )


def split_heads(row_matrix, head_group):
    begin = head_group * heads_block * HEAD_DIM
    piece = row_matrix[:, begin : begin + heads_block * HEAD_DIM]
    return piece.reshape(row_matrix.shape[0], heads_block, HEAD_DIM)


def join_heads(parts_list):
    return jnp.concatenate(
        [part_one.reshape(part_one.shape[0], heads_block * HEAD_DIM) for part_one in parts_list],
        axis=1,
    )


def attend_forward(query_rows, key_all, value_all, query_pos, key_pos):
    score_scale = HEAD_DIM ** (-0.5)
    allowed = (query_pos[:, None] >= key_pos[None, :])[None]
    head_outs = []
    log_sums = []
    for head_group in range(HEADS // heads_block):
        q_heads = split_heads(query_rows, head_group)
        k_heads = split_heads(key_all, head_group)
        v_heads = split_heads(value_all, head_group)
        scores = (
            jnp.einsum("qhd,khd->hqk", q_heads, k_heads, preferred_element_type=jnp.float32)
            * score_scale
        )
        scores = jnp.where(allowed, scores, masked_score)
        row_peak = jnp.max(scores, axis=-1, keepdims=True)
        row_total = jnp.sum(jnp.exp(scores - row_peak), axis=-1, keepdims=True)
        log_total = row_peak + jnp.log(row_total)
        prob_rows = jnp.exp(scores - log_total).astype(jnp.bfloat16)
        head_outs.append(
            jnp.einsum("hqk,khd->qhd", prob_rows, v_heads, preferred_element_type=jnp.float32)
        )
        log_sums.append(log_total[..., 0])
    return (join_heads(head_outs), jnp.concatenate(log_sums, axis=0))


def attend_query_back(query_rows, key_all, value_all, grad_rows, log_sums, query_pos, key_pos):
    score_scale = HEAD_DIM ** (-0.5)
    allowed = (query_pos[:, None] >= key_pos[None, :])[None]
    grad_q_parts = []
    delta_parts = []
    grad_k_parts = []
    grad_v_parts = []
    for head_group in range(HEADS // heads_block):
        head_span = slice(head_group * heads_block, (head_group + 1) * heads_block)
        q_heads = split_heads(query_rows, head_group)
        k_heads = split_heads(key_all, head_group)
        v_heads = split_heads(value_all, head_group)
        g_heads = split_heads(grad_rows, head_group)
        scores = (
            jnp.einsum("qhd,khd->hqk", q_heads, k_heads, preferred_element_type=jnp.float32)
            * score_scale
        )
        scores = jnp.where(allowed, scores, masked_score)
        prob_rows = jnp.exp(scores - log_sums[head_span][:, :, None])
        grad_prob = jnp.einsum("qhd,khd->hqk", g_heads, v_heads, preferred_element_type=jnp.float32)
        row_delta = jnp.sum(prob_rows * grad_prob, axis=-1)
        grad_score = (prob_rows * (grad_prob - row_delta[:, :, None])).astype(jnp.bfloat16)
        grad_q_parts.append(
            jnp.einsum("hqk,khd->qhd", grad_score, k_heads, preferred_element_type=jnp.float32)
            * score_scale
        )
        delta_parts.append(row_delta)
        grad_k_parts.append(
            jnp.einsum("hqk,qhd->khd", grad_score, q_heads, preferred_element_type=jnp.float32)
            * score_scale
        )
        grad_v_parts.append(
            jnp.einsum(
                "hqk,qhd->khd",
                prob_rows.astype(jnp.bfloat16),
                g_heads,
                preferred_element_type=jnp.float32,
            )
        )
    return (
        join_heads(grad_q_parts),
        jnp.concatenate(delta_parts, axis=0),
        join_heads(grad_k_parts),
        join_heads(grad_v_parts),
    )


def project(flat_bf, w_attn, vector, seq_here):
    query_rows = (matmul(flat_bf, w_attn[0]) + vector[0]).astype(jnp.bfloat16)
    key_rows = matmul(flat_bf, w_attn[1]).astype(jnp.bfloat16)
    value_rows = (matmul(flat_bf, w_attn[2]) + vector[1]).astype(jnp.bfloat16)
    return (
        query_rows.reshape(seq_here, -1, D),
        key_rows.reshape(seq_here, -1, D),
        value_rows.reshape(seq_here, -1, D),
    )


def dense_part(flat_rows, heads_bf, w_out, w_in, w_down, vector):
    branch = matmul(heads_bf, w_out) + vector[2]
    first_norm = layer_norm(flat_rows + branch, vector[4], vector[5])
    first_bf = first_norm.astype(jnp.bfloat16)
    inner_pre = matmul(first_bf, w_in) + vector[8:].reshape(-1)
    activated = gelu_exact(inner_pre).astype(jnp.bfloat16)
    feed_out = matmul(activated, w_down) + vector[3]
    second_sum = first_norm + feed_out
    output = layer_norm(second_sum, vector[6], vector[7])
    return (branch, first_norm, first_bf, inner_pre, activated, feed_out, second_sum, output)


def body(
    hidden_in,
    block_of,
    lengths,
    attn_latent,
    ffn_in_latent,
    ffn_out_latent,
    student_vec,
    teacher_attn,
    teacher_ffn_in,
    teacher_ffn_out,
    teacher_vec,
):
    seq_here, rows_here = (hidden_in.shape[0], hidden_in.shape[1])
    token_count = seq_here * rows_here
    ctx_index = lax.axis_index("ctx")
    shard_index = lax.axis_index("shard")
    key_pos = positions_of(block_of)
    query_pos = lax.dynamic_slice_in_dim(key_pos, ctx_index * rows_here, rows_here)
    own_lengths = lax.dynamic_slice_in_dim(lengths, shard_index * seq_here, seq_here)
    valid_rows = (
        (query_pos[None, :] < own_lengths[:, None]).astype(jnp.float32).reshape(token_count, 1)
    )
    valid_count = jnp.sum(lengths.astype(jnp.float32))
    loss_scale = valid_count * D
    attn_gain = jnp.asarray(attn_gains, dtype=jnp.float32)[:, None, None]
    full_attn, full_in, full_out = (
        lax.all_gather(attn_latent, "shard", axis=1, tiled=True),
        lax.all_gather(ffn_in_latent, "shard", axis=0, tiled=True),
        lax.all_gather(ffn_out_latent, "shard", axis=0, tiled=True),
    )
    bin_attn = binarize(full_attn, jnp.sum(jnp.abs(full_attn), axis=1, keepdims=True), attn_gain, D)
    bin_in = binarize(full_in, jnp.sum(jnp.abs(full_in), axis=0, keepdims=True), 1.0, D)
    bin_out = binarize(full_out, jnp.sum(jnp.abs(full_out), axis=0, keepdims=True), 1.0, FF)
    teach_attn, teach_in, teach_out = (
        lax.all_gather(teacher_attn, "shard", axis=1, tiled=True),
        lax.all_gather(teacher_ffn_in, "shard", axis=0, tiled=True),
        lax.all_gather(teacher_ffn_out, "shard", axis=0, tiled=True),
    )
    flat_bf = hidden_in.reshape(token_count, D)
    flat_rows = flat_bf.astype(jnp.float32)
    s_query, s_key, s_value = project(flat_bf, bin_attn, student_vec, seq_here)
    t_query, t_key, t_value = project(flat_bf, teach_attn, teacher_vec, seq_here)
    key_all, value_all, t_key_all, t_value_all = (
        lax.all_gather(s_key, "ctx", axis=1, tiled=True),
        lax.all_gather(s_value, "ctx", axis=1, tiled=True),
        lax.all_gather(t_key, "ctx", axis=1, tiled=True),
        lax.all_gather(t_value, "ctx", axis=1, tiled=True),
    )

    def forward_seq(seq_item):
        return attend_forward(seq_item[0], seq_item[1], seq_item[2], query_pos, key_pos)

    t_heads = lax.map(forward_seq, (t_query, t_key_all, t_value_all))[0]
    t_parts = dense_part(
        flat_rows,
        t_heads.reshape(token_count, D).astype(jnp.bfloat16),
        teach_attn[3],
        teach_in,
        teach_out,
        teacher_vec,
    )
    target = t_parts[7]
    s_heads, s_lse = lax.map(forward_seq, (s_query, key_all, value_all))
    heads_bf = s_heads.reshape(token_count, D).astype(jnp.bfloat16)
    branch, first_norm, first_bf, inner_pre, activated, feed_out, second_sum, output = dense_part(
        flat_rows, heads_bf, bin_attn[3], bin_in, bin_out, student_vec
    )
    mismatch = output - target
    grad_output = valid_rows * mismatch / loss_scale
    second_back = jax.vjp(layer_norm, second_sum, student_vec[6], student_vec[7])[1]
    grad_second, grad_g2, grad_c2 = second_back(grad_output)
    grad_b2 = jnp.sum(grad_second, axis=0)
    feed_bf = grad_second.astype(jnp.bfloat16)
    grad_down = left_product(activated, feed_bf)
    grad_act = right_product(feed_bf, bin_out)
    grad_inner = jax.vjp(gelu_exact, inner_pre)[1](grad_act)[0]
    grad_b1 = jnp.sum(grad_inner, axis=0)
    inner_bf = grad_inner.astype(jnp.bfloat16)
    grad_in = left_product(first_bf, inner_bf)
    grad_first = grad_second + right_product(inner_bf, bin_in)
    first_back = jax.vjp(layer_norm, flat_rows + branch, student_vec[4], student_vec[5])[1]
    grad_res, grad_g1, grad_c1 = first_back(grad_first)
    grad_bo = jnp.sum(grad_res, axis=0)
    branch_bf = grad_res.astype(jnp.bfloat16)
    grad_wo = left_product(heads_bf, branch_bf)
    grad_heads = (
        right_product(branch_bf, bin_attn[3]).astype(jnp.bfloat16).reshape(seq_here, rows_here, D)
    )

    def back_seq(seq_item):
        return attend_query_back(
            seq_item[0], seq_item[1], seq_item[2], seq_item[3], seq_item[4], query_pos, key_pos
        )

    grad_query, row_deltas, key_part, value_part = lax.map(
        back_seq, (s_query, key_all, value_all, grad_heads, s_lse)
    )
    grad_key, grad_value = (
        lax.psum_scatter(
            key_part.astype(jnp.bfloat16), "ctx", scatter_dimension=1, tiled=True
        ).astype(jnp.float32),
        lax.psum_scatter(
            value_part.astype(jnp.bfloat16), "ctx", scatter_dimension=1, tiled=True
        ).astype(jnp.float32),
    )
    grad_query = grad_query.reshape(token_count, D)
    grad_key = grad_key.reshape(token_count, D)
    grad_value = grad_value.reshape(token_count, D)
    grad_bq = jnp.sum(grad_query, axis=0)
    grad_bv = jnp.sum(grad_value, axis=0)
    query_bf = grad_query.astype(jnp.bfloat16)
    key_bf = grad_key.astype(jnp.bfloat16)
    value_bf = grad_value.astype(jnp.bfloat16)
    grad_attn = jnp.stack(
        [
            left_product(flat_bf, query_bf),
            left_product(flat_bf, key_bf),
            left_product(flat_bf, value_bf),
            grad_wo,
        ]
    )
    grad_flat = (
        grad_res
        + right_product(query_bf, bin_attn[0])
        + right_product(key_bf, bin_attn[1])
        + right_product(value_bf, bin_attn[2])
    )
    red_attn, red_in, red_down = (
        lax.psum_scatter(
            grad_attn.astype(jnp.bfloat16), "shard", scatter_dimension=1, tiled=True
        ).astype(jnp.float32),
        lax.psum_scatter(
            grad_in.astype(jnp.bfloat16), "shard", scatter_dimension=0, tiled=True
        ).astype(jnp.float32),
        lax.psum_scatter(
            grad_down.astype(jnp.bfloat16), "shard", scatter_dimension=0, tiled=True
        ).astype(jnp.float32),
    )
    red_attn, red_in, red_down = (
        lax.psum(red_attn.astype(jnp.bfloat16), "ctx").astype(jnp.float32),
        lax.psum(red_in.astype(jnp.bfloat16), "ctx").astype(jnp.float32),
        lax.psum(red_down.astype(jnp.bfloat16), "ctx").astype(jnp.float32),
    )
    keep_attn = (jnp.abs(attn_latent) <= 1.0).astype(jnp.float32)
    keep_in = (jnp.abs(ffn_in_latent) <= 1.0).astype(jnp.float32)
    keep_out = (jnp.abs(ffn_out_latent) <= 1.0).astype(jnp.float32)
    vec_grad = jnp.concatenate(
        [
            jnp.stack([grad_bq, grad_bv, grad_bo, grad_b2, grad_g1, grad_c1, grad_g2, grad_c2]),
            grad_b1.reshape(-1, D),
        ],
        axis=0,
    )
    square_sums = jnp.stack(
        [
            0.5 * jnp.sum(valid_rows * mismatch * mismatch),
            jnp.sum(valid_rows * branch * branch),
            jnp.sum(valid_rows * feed_out * feed_out),
            jnp.sum(valid_rows * second_sum * second_sum),
        ]
    )
    vec_total, sum_total = lax.psum((vec_grad, square_sums), ("ctx", "shard"))
    statistics = jnp.concatenate(
        [sum_total[0:1] / loss_scale, jnp.sqrt(sum_total[1:] / loss_scale)]
    )
    return (
        output.reshape(seq_here, rows_here, D).astype(jnp.bfloat16),
        statistics,
        grad_flat.reshape(seq_here, rows_here, D),
        red_attn * keep_attn,
        red_in * keep_in,
        red_down * keep_out,
        vec_total[1:],
        vec_total[0],
    )


def solution(mesh):
    in_specs = (
        P("shard", "ctx", None),
        P(),
        P(),
        P(None, "shard", None),
        P("shard", None),
        P("shard", None),
        P(),
        P(None, "shard", None),
        P("shard", None),
        P("shard", None),
        P(),
    )
    out_specs = (
        P("shard", "ctx", None),
        P(),
        P("shard", "ctx", None),
        P(None, "shard", None),
        P("shard", None),
        P("shard", None),
        P(),
        P(),
    )
    return jax.shard_map(body, mesh=mesh, in_specs=in_specs, out_specs=out_specs, check_vma=False)
```

profile of v0, /device:TPU:0, one launch (start us, length us, event | category | flops | bytes accessed | tf_op | source)
XLA Modules:
  0.0 1617.2 jit_solution(1807778586871363878)
XLA Ops:
  9.4 92.4 %all-gather.21.cloned.1.call-done = bf16[4,768,768]{2,1,0:T(8,128)(2,1)} async-done(((bf16[4,192,768]{2,1,0:T(8,128)(2,1)}), bf16[4,768,768]{2,1,0:T(8,128)(2,1)}) %all-gather.21.cloned.1.call-update) | async-done | bytes 4718608 | tf_op jit(solution)/shard_map/all_gather | solution.py:197
  116.7 151.8 %all-gather.11.cloned.1.call-done = f32[4,768,768]{2,1,0:T(8,128)} async-done(((f32[4,192,768]{2,1,0:T(8,128)}), f32[4,768,768]{2,1,0:T(8,128)}) %all-gather.11.cloned.1.call-update) | async-done | bytes 9437200 | tf_op jit(solution)/shard_map/all_gather | solution.py:189
  268.6 4.5 abs_reduce_fusion.2
  282.0 20.1 %all-gather.23.cloned.1.call-done = bf16[2,1024,768]{1,2,0:T(8,128)(2,1)} async-done(((bf16[2,128,768]{1,2,0:T(8,128)(2,1)}), bf16[2,1024,768]{1,2,0:T(8,128)(2,1)}) %all-gather.23.cloned.1.call-update) | async-done | bytes 3145744 | tf_op jit(solution)/shard_map/all_gather | solution.py:209
  302.1 35.2 %all-gather.25.cloned.1.call-done = bf16[2,1024,768]{1,2,0:T(8,128)(2,1)} async-done(((bf16[2,128,768]{1,2,0:T(8,128)(2,1)}), bf16[2,1024,768]{1,2,0:T(8,128)(2,1)}) %all-gather.25.cloned.1.call-update) | async-done | bytes 3145744 | tf_op jit(solution)/shard_map/all_gather | solution.py:208
  338.0 20.3 %while.40 = (s32[]{:T(128)}, bf16[2,128,768]{2,1,0:T(8,128)(2,1)}, bf16[2,1024,768]{1,2,0:T(8,128)(2,1)}, s32[128]{0:T(128)S(1)}, bf16[2,128,768]{2,1,0:T(8,128)...) while((s32[]{:T(128)}, bf16[2,128,768]{2,1,0:T(8,128)(2,1)}, ...), condition=%wide.region_22.23_spmd.clone, body=%wide.region_15.22_spmd.clone.sunk | while | flops 414383616 | bytes 42658548 | solution.py:215
  363.9 64.1 %all-gather.27.cloned.1.call-done = bf16[768,3072]{1,0:T(8,128)(2,1)} async-done(((bf16[192,3072]{1,0:T(8,128)(2,1)}), bf16[768,3072]{1,0:T(8,128)(2,1)}) %all-gather.27.cloned.1.call-update) | async-done | bytes 4718608 | tf_op jit(solution)/shard_map/all_gather | solution.py:198
  428.1 89.4 %all-gather.29.cloned.1.call-done = bf16[3072,768]{1,0:T(8,128)(2,1)} async-done(((bf16[768,768]{1,0:T(8,128)(2,1)}), bf16[3072,768]{1,0:T(8,128)(2,1)}) %all-gather.29.cloned.1.call-update) | async-done | bytes 4718608 | tf_op jit(solution)/shard_map/all_gather | solution.py:199
  517.5 13.0 fusion.146
  533.3 150.9 %all-gather.19.cloned.1.call-done = f32[3072,768]{1,0:T(8,128)} async-done(((f32[768,768]{1,0:T(8,128)}), f32[3072,768]{1,0:T(8,128)}) %all-gather.19.cloned.1.call-update) | async-done | bytes 9437200 | tf_op jit(solution)/shard_map/all_gather | solution.py:191
  684.3 4.5 abs_reduce_fusion
  689.4 161.5 %all-gather.17.cloned.1.call-done = f32[768,3072]{1,0:T(8,128)} async-done(((f32[192,3072]{1,0:T(8,128)}), f32[768,3072]{1,0:T(8,128)}) %all-gather.17.cloned.1.call-update) | async-done | bytes 9437200 | tf_op jit(solution)/shard_map/all_gather | solution.py:190
  850.8 4.5 abs_reduce_fusion.1
  855.9 28.4 %all-gather.13.cloned.1.call-done = bf16[2,1024,768]{1,2,0:T(8,128)(2,1)} async-done(((bf16[2,128,768]{1,2,0:T(8,128)(2,1)}), bf16[2,1024,768]{1,2,0:T(8,128)(2,1)}) %all-gather.13.cloned.1.call-update) | async-done | bytes 3145744 | tf_op jit(solution)/shard_map/all_gather | solution.py:207
  884.3 35.3 %all-gather.15.cloned.1.call-done = bf16[2,1024,768]{1,2,0:T(8,128)(2,1)} async-done(((bf16[2,128,768]{1,2,0:T(8,128)(2,1)}), bf16[2,1024,768]{1,2,0:T(8,128)(2,1)}) %all-gather.15.cloned.1.call-update) | async-done | bytes 3145744 | tf_op jit(solution)/shard_map/all_gather | solution.py:206
  920.4 22.6 %while.39 = (s32[]{:T(128)}, bf16[2,128,768]{2,1,0:T(8,128)(2,1)}, f32[2,12,128]{2,1,0:T(8,128)}, bf16[2,1024,768]{1,2,0:T(8,128)(2,1)}, s32[128]{0:T(128)S(1)},...) while((s32[]{:T(128)}, bf16[2,128,768]{2,1,0:T(8,128)(2,1)}, ...), condition=%wide.region_8.9_spmd.clone, body=%wide.region_1.8_spmd.clone.sunk | while | flops 414386688 | bytes 41334212 | solution.py:225
  945.6 13.0 multiply_convert_fusion.6
  958.8 3.7 fusion.126
  965.5 11.6 fusion.149
  977.2 4.3 multiply_reduce_fusion.4
  984.6 79.8 %while.41 = (s32[]{:T(128)}, f32[2,128,768]{1,2,0:T(8,128)}, bf16[2,1024,768]{2,1,0:T(8,128)(2,1)}, bf16[2,1024,768]{2,1,0:T(8,128)(2,1)}, bf16[2,1024,768]{1,2,...) while((s32[]{:T(128)}, f32[2,128,768]{1,2,0:T(8,128)}, ...), condition=%wide.region_41.42_spmd.clone, body=%wide.region_37.41_spmd.clone.sunk | while | flops 1032224256 | bytes 197981808 | solution.py:257
  1068.5 42.3 %reduce-scatter.5.cloned.1.call-done = bf16[2,128,768]{2,1,0:T(8,128)(2,1)} async-done(((bf16[2,1024,768]{2,1,0:T(8,128)(2,1)}), bf16[2,128,768]{2,1,0:T(8,128)(2,1)}) %reduce-scatter.5.cloned.1.call-update) | async-done | bytes 393232 | tf_op jit(solution)/shard_map/reduce_scatter | solution.py:261
  1113.3 47.4 %reduce-scatter.7.cloned.1.call-done = bf16[2,128,768]{2,1,0:T(8,128)(2,1)} async-done(((bf16[2,1024,768]{2,1,0:T(8,128)(2,1)}), bf16[2,128,768]{2,1,0:T(8,128)(2,1)}) %reduce-scatter.7.cloned.1.call-update) | async-done | bytes 393232 | tf_op jit(solution)/shard_map/reduce_scatter | solution.py:264
  1162.2 3.7 pad_maximum_fusion
  1165.9 8.6 copy.68
  1175.6 5.3 convolution_convert_fusion
  1182.1 5.1 convolution_convert_fusion.1
  1189.1 157.5 %all-reduce.6.cloned.1.call-done = bf16[4,768,768]{2,0,1:T(4,128)(2,1)} async-done(((bf16[4,768,768]{2,0,1:T(4,128)(2,1)}), bf16[4,768,768]{2,0,1:T(4,128)(2,1)}) %all-reduce.6.cloned.1.call-update) | async-done | bytes 4718608
  1349.3 83.7 %reduce-scatter.11.cloned.1.call-done = bf16[768,768]{1,0:T(8,128)(2,1)} async-done(((bf16[3072,768]{1,0:T(8,128)(2,1)}), bf16[768,768]{1,0:T(8,128)(2,1)}) %reduce-scatter.11.cloned.1.call-update) | async-done | bytes 1179664 | tf_op jit(solution)/shard_map/reduce_scatter | solution.py:297
  1433.1 88.0 %reduce-scatter.9.cloned.1.call-done = bf16[192,3072]{1,0:T(8,128)(2,1)} async-done(((bf16[768,3072]{1,0:T(8,128)(2,1)}), bf16[192,3072]{1,0:T(8,128)(2,1)}) %reduce-scatter.9.cloned.1.call-update) | async-done | bytes 1179664 | tf_op jit(solution)/shard_map/reduce_scatter | solution.py:294
  1528.2 41.8 %all-reduce.1 = (f32[4]{0:T(128)S(1)}, f32[12,768]{1,0:T(8,128)S(1)}) all-reduce(f32[4]{0:T(128)S(1)} %pad_maximum_fusion.1, f32[12,768]{1,0:T(8,128)S(1)} %concatenate.25), channel_id=1, replica_groups=mesh['ctx'=8,'shard'=4] {'ctx','shard'}, use_global_device_ids=true, to_apply=%region_31.32 | all-reduce | flops 9220 | bytes 73760 | tf_op jit(solution)/shard_map/psum | solution.py:324
  1576.8 23.8 %all-reduce.8.cloned.1.call-done = (bf16[4,192,768]{2,0,1:T(4,128)(2,1)}, bf16[192,3072]{1,0:T(8,128)(2,1)}, bf16[768,768]{1,0:T(8,128)(2,1)}) async-done(((bf16[4,192,768]{2,0,1:T(4,128)(2,1)}, bf16[192,3072]{1,0:T(8,128)(2,1)}, bf16[768,768]{1,0:T(8,128)(2,1)}), (bf16[4,192,768]{2,0,1:T(4,128)(2,1)}, bf16[192,3072]{1,0:T(8,128)(2,1)}, bf16[768,768]{1,0:T(8,128)(2,1)})) %all-reduce.8.cloned.1.call-update) | async-done | bytes 3538960 | tf_op jit(solution)/shard_map/psum | solution.py:302
  (599 shorter events, 202.9 us)
Async XLA Ops:
  7.2 94.6 %copy-start.34 = (bf16[2,128,768]{2,1,0:T(8,128)(2,1)S(1)}, bf16[2,128,768]{2,1,0:T(8,128)(2,1)}, u32[]{:S(2)}) copy-start(bf16[2,128,768]{2,1,0:T(8,128)(2,1)} %param.18) | copy-start | bytes 1179652
  7.2 94.5 %all-gather.21.cloned.1.call-start = ((), (), s32[]{:S(2)}) async-start(), calls=%async_computation.9 | async-start | bytes 5898240 | tf_op jit(solution)/shard_map/all_gather | solution.py:197
  7.9 260.6 %all-gather.11.cloned.1.call-start = ((), (), s32[]{:S(2)}) async-start(), calls=%async_computation.4 | async-start | bytes 11796480 | tf_op jit(solution)/shard_map/all_gather | solution.py:189
  8.7 293.4 %all-gather.23.cloned.1.call-start = ((), (), s32[]{:S(2)}) async-start(), calls=%async_computation.10 | async-start | bytes 3538944 | tf_op jit(solution)/shard_map/all_gather | solution.py:209
  104.4 232.8 %all-gather.25.cloned.1.call-start = ((), (), s32[]{:S(2)}) async-start(), calls=%async_computation.11 | async-start | bytes 3538944 | tf_op jit(solution)/shard_map/all_gather | solution.py:208
  107.2 320.9 %all-gather.27.cloned.1.call-start = ((), (), s32[]{:S(2)}) async-start(), calls=%async_computation.12 | async-start | bytes 5898240 | tf_op jit(solution)/shard_map/all_gather | solution.py:198
  107.8 409.6 %all-gather.29.cloned.1.call-start = ((), (), s32[]{:S(2)}) async-start(), calls=%async_computation.13 | async-start | bytes 5898240 | tf_op jit(solution)/shard_map/all_gather | solution.py:199
  108.4 575.9 %all-gather.19.cloned.1.call-start = ((), (), s32[]{:S(2)}) async-start(), calls=%async_computation.8 | async-start | bytes 11796480 | tf_op jit(solution)/shard_map/all_gather | solution.py:191
  109.2 741.7 %all-gather.17.cloned.1.call-start = ((), (), s32[]{:S(2)}) async-start(), calls=%async_computation.7 | async-start | bytes 11796480 | tf_op jit(solution)/shard_map/all_gather | solution.py:190
  109.9 774.4 %all-gather.13.cloned.1.call-start = ((), (), s32[]{:S(2)}) async-start(), calls=%async_computation.5 | async-start | bytes 3538944 | tf_op jit(solution)/shard_map/all_gather | solution.py:207
  113.5 868.0 %copy-start.55 = (f32[768]{0:T(1024)}, f32[768]{0:T(1024)S(1)}, u32[]{:S(2)}) copy-start(f32[768]{0:T(1024)S(1)} %get-tuple-element.337) | copy-start | bytes 9220
  116.7 156.3 %copy-start.101 = (f32[4]{0:T(128)S(1)}, f32[4]{0:T(128)}, u32[]{:S(2)}) copy-start(f32[4]{0:T(128)} %constant.192) | copy-start | bytes 52
  281.6 638.0 %all-gather.15.cloned.1.call-start = ((), (), s32[]{:S(2)}) async-start(), calls=%async_computation.6 | async-start | bytes 3538944 | tf_op jit(solution)/shard_map/all_gather | solution.py:206
  358.3 159.1 %copy-start.85 = (f32[3072]{0:T(1024)S(1)}, f32[3072]{0:T(1024)}, u32[]{:S(2)}) copy-start(f32[3072]{0:T(1024)} %add.353) | copy-start | bytes 36868
  358.3 159.1 %copy-start.94 = (f32[768]{0:T(1024)S(1)}, f32[768]{0:T(1024)}, u32[]{:S(2)}) copy-start(f32[768]{0:T(1024)} %get-tuple-element.327) | copy-start | bytes 9220
  358.3 159.1 %copy-start.95 = (f32[768]{0:T(1024)S(1)}, f32[768]{0:T(1024)}, u32[]{:S(2)}) copy-start(f32[768]{0:T(1024)} %get-tuple-element.328) | copy-start | bytes 9220
  358.4 159.1 %copy-start.96 = (f32[768]{0:T(1024)S(1)}, f32[768]{0:T(1024)}, u32[]{:S(2)}) copy-start(f32[768]{0:T(1024)} %get-tuple-element.329) | copy-start | bytes 9220
  361.3 749.5 %reduce-scatter.5.cloned.1.call-start = ((), (), s32[]{:S(2)}) async-start(), calls=%async_computation.14 | async-start | bytes 3538944 | tf_op jit(solution)/shard_map/reduce_scatter | solution.py:261
  530.4 158.3 %copy-start.42 = (f32[256,768]{1,0:T(8,128)}, f32[256,768]{1,0:T(8,128)S(1)}, u32[]{:S(2)}) copy-start(f32[256,768]{1,0:T(8,128)S(1)} %get-tuple-element.475) | copy-start | bytes 2359300
  945.3 36.3 %copy-start.21 = (f32[256,768]{1,0:T(8,128)}, f32[256,768]{1,0:T(8,128)S(1)}, u32[]{:S(2)}) copy-start(f32[256,768]{1,0:T(8,128)S(1)} %get-tuple-element.409) | copy-start | bytes 2359300
  1064.4 96.3 %reduce-scatter.7.cloned.1.call-start = ((), (), s32[]{:S(2)}) async-start(), calls=%async_computation.15 | async-start | bytes 3538944 | tf_op jit(solution)/shard_map/reduce_scatter | solution.py:264
  1065.0 281.6 %all-reduce.6.cloned.1.call-start = ((), (), s32[]{:S(2)}) async-start(), calls=%async_computation.18 | async-start | bytes 9437184
  1174.5 258.6 %reduce-scatter.11.cloned.1.call-start = ((), (), s32[]{:S(2)}) async-start(), calls=%async_computation.17 | async-start | bytes 5898240 | tf_op jit(solution)/shard_map/reduce_scatter | solution.py:297
  1181.0 340.0 %reduce-scatter.9.cloned.1.call-start = ((), (), s32[]{:S(2)}) async-start(), calls=%async_computation.16 | async-start | bytes 5898240 | tf_op jit(solution)/shard_map/reduce_scatter | solution.py:294
  1187.3 413.3 %all-reduce.8.cloned.1.call-start = ((), (), s32[]{:S(2)}) async-start(), calls=%async_computation.19 | async-start | bytes 7077888 | tf_op jit(solution)/shard_map/psum | solution.py:302
  1349.3 173.4 %copy-start.99 = (f32[768]{0:T(1024)S(1)}, f32[768]{0:T(1024)}, u32[]{:S(2)}) copy-start(f32[768]{0:T(1024)} %get-tuple-element.318) | copy-start | bytes 9220
  1349.3 173.4 %copy-start.98 = (f32[768]{0:T(1024)S(1)}, f32[768]{0:T(1024)}, u32[]{:S(2)}) copy-start(f32[768]{0:T(1024)} %get-tuple-element.325) | copy-start | bytes 9220
  1349.3 173.4 %copy-start.84 = (f32[3072]{0:T(1024)S(1)}, f32[3072]{0:T(1024)}, u32[]{:S(2)}) copy-start(f32[3072]{0:T(1024)} %get-tuple-element.477) | copy-start | bytes 36868
  1349.3 173.4 %copy-start.80 = (f32[768]{0:T(1024)S(1)}, f32[768]{0:T(1024)}, u32[]{:S(2)}) copy-start(f32[768]{0:T(1024)} %get-tuple-element.323) | copy-start | bytes 9220
  1349.3 173.5 %copy-start.79 = (f32[768]{0:T(1024)S(1)}, f32[768]{0:T(1024)}, u32[]{:S(2)}) copy-start(f32[768]{0:T(1024)} %get-tuple-element.320) | copy-start | bytes 9220
  1349.3 176.0 %copy-start.37 = (bf16[2,128,768]{2,1,0:T(8,128)(2,1)S(1)}, bf16[2,128,768]{2,1,0:T(8,128)(2,1)}, u32[]{:S(2)}) copy-start(bf16[2,128,768]{2,1,0:T(8,128)(2,1)} %reduce-scatter.7.cloned.1.call-done) | copy-start | bytes 1179652
  1521.0 50.9 %copy-start.47 = (bf16[2,128,768]{2,1,0:T(8,128)(2,1)S(1)}, bf16[2,128,768]{2,1,0:T(8,128)(2,1)}, u32[]{:S(2)}) copy-start(bf16[2,128,768]{2,1,0:T(8,128)(2,1)} %reduce-scatter.5.cloned.1.call-done) | copy-start | bytes 1179652
  (138 other events, 579.8 us)
Sparse Core Ops, SparseCore 0:
  9.6 92.0 all-gather.20
  103.3 165.2 all-gather.10
  271.0 30.9 all-gather.22
  304.4 32.8 all-gather.24
  338.6 89.4 all-gather.26
  429.5 87.8 all-gather.28
  519.0 165.2 all-gather.18
  685.8 164.9 all-gather.16
  853.3 30.9 all-gather.12
  886.6 32.8 all-gather.14
  1064.5 46.2 reduce-scatter.4
  1114.4 46.2 reduce-scatter.6
  1174.6 171.9 all-reduce.5
  1348.8 84.2 reduce-scatter.10
  1435.2 85.7 reduce-scatter.8
  1525.1 75.4 all-reduce.7
where the time goes:
time: 1620 us
  waiting for transfers between devices  1280 us (79%)
  matrix products  118 us (7%)
  local copies, waits for them, and re-layouts  99.5 us (6%)
  other arithmetic  60.8 us (4%)
  blocking collectives  41.8 us (3%)
  between operations  17.2 us (1%)
    unnamed x17, waiting for transfers between devices  162 us
    all_gather x1, waiting for transfers between devices, body(): lax.all_gather(ffn_in_latent, 'shard', axis=0, tiled=True)  161 us
    all_gather x1, waiting for transfers between devices, body(): lax.all_gather(attn_latent, 'shard', axis=1, tiled=True)  152 us
    all_gather x1, waiting for transfers between devices, body(): lax.all_gather(ffn_out_latent, 'shard', axis=0, tiled=True)  151 us
    all_gather x1, waiting for transfers between devices, body(): lax.all_gather(teacher_attn, 'shard', axis=1, tiled=True)  92.4 us
    all_gather x1, waiting for transfers between devices, body(): lax.all_gather(teacher_ffn_out, 'shard', axis=0, tiled=True)  89.4 us
    reduce_scatter x1, waiting for transfers between devices, body(): lax.psum_scatter(grad_in.astype(jnp.bfloat16), 'shard', scatter_dimension...  88 us
    reduce_scatter x1, waiting for transfers between devices, body(): lax.psum_scatter(grad_down.astype(jnp.bfloat16), 'shard', scatter_dimensi...  83.7 us
  transfers between devices with their start and end apart: 16, of which 16 were waited for; matrix products, arithmetic and copies ran while one was open for 6% of the time, Pallas kernels for 0%

commit v1 on v0

--- a/solution.py
+++ b/solution.py
@@ -1,3 +1,4 @@
+import functools
 import jax
 import jax.numpy as jnp
 from jax import lax
@@ -12,6 +13,21 @@
 attn_gains = (2.0, 2.0, 1.0, 4.0)
 heads_block = 4
 masked_score = -1e30
+
+
+def list_slabs(x_part, dev_axis, at_axis):
+    opened, all_values = (lax.axis_size(dev_axis), lax.axis_index(dev_axis))
+    small, frame_out = (x_part, 1)
+    while frame_out < opened:
+        vec_out = lax.ppermute(small, dev_axis, [(pp, pp ^ frame_out) for pp in range(opened)])
+        block_out = jnp.concatenate([small, vec_out], axis=at_axis)
+        earlier = jnp.concatenate([vec_out, small], axis=at_axis)
+        small = jnp.where(all_values & frame_out == 0, block_out, earlier)
+        frame_out = 2 * frame_out
+    return small
+
+
+views_compute = functools.partial(list_slabs, dev_axis="shard", at_axis=0)
 
 
 def layer_norm(values, gain, shift):
@@ -188,7 +204,7 @@
     full_attn, full_in, full_out = (
         lax.all_gather(attn_latent, "shard", axis=1, tiled=True),
         lax.all_gather(ffn_in_latent, "shard", axis=0, tiled=True),
-        lax.all_gather(ffn_out_latent, "shard", axis=0, tiled=True),
+        views_compute(ffn_out_latent),
     )
     bin_attn = binarize(full_attn, jnp.sum(jnp.abs(full_attn), axis=1, keepdims=True), attn_gain, D)
     bin_in = binarize(full_in, jnp.sum(jnp.abs(full_in), axis=0, keepdims=True), 1.0, D)

time: 1620 us -> 1560 us (0.963)
  waiting for transfers between devices: 1280 us -> 1230 us
  local copies, waits for them, and re-layouts: 99.5 us -> 71.8 us
    ppermute x0 -> x2, waiting for transfers between devices: none -> 481 us  [list_slabs(): lax.ppermute(small, dev_axis, [(pp, pp ^ frame_out) for pp in range(opene...]
    all_gather x1 -> x0, waiting for transfers between devices: 151 us -> none  [body(): lax.all_gather(ffn_out_latent, 'shard', axis=0, tiled=True)]
    all_gather x1, waiting for transfers between devices: 152 us -> 40.7 us  [body(): lax.all_gather(attn_latent, 'shard', axis=1, tiled=True)]
    all_gather x1, waiting for transfers between devices: 89.4 us -> 0.02 us  [body(): lax.all_gather(teacher_ffn_out, 'shard', axis=0, tiled=True)]
    all_gather x1, waiting for transfers between devices: 64.1 us -> 0.02 us  [body(): lax.all_gather(teacher_ffn_in, 'shard', axis=0, tiled=True)]
    all_gather x1, waiting for transfers between devices: 161 us -> 114 us  [body(): lax.all_gather(ffn_in_latent, 'shard', axis=0, tiled=True)]
    all_gather x1, waiting for transfers between devices: 35.2 us -> 0.02 us  [body(): lax.all_gather(t_key, 'ctx', axis=1, tiled=True)]
    all_gather x1, waiting for transfers between devices: 20.1 us -> 0.02 us  [body(): lax.all_gather(t_value, 'ctx', axis=1, tiled=True)]
  transfers between devices with their start and end apart: 16 -> 17, of which waited for: 16 -> 13; matrix products, arithmetic and copies ran while one was open for 6% -> 8% of each run, Pallas kernels for 0% -> 0%
where the time goes in v1:
time: 1560 us; the launch traced here: 1550 us
  waiting for transfers between devices  1230 us (79%)
  matrix products  110 us (7%)
  other arithmetic  74 us (5%)
  local copies, waits for them, and re-layouts  71.8 us (5%)
  blocking collectives  41.7 us (3%)
  between operations  17.3 us (1%)
    ppermute x2, waiting for transfers between devices, list_slabs(): lax.ppermute(small, dev_axis, [(pp, pp ^ frame_out) for pp in range(opene...  481 us
    unnamed x16, waiting for transfers between devices  162 us
    all_gather x1, waiting for transfers between devices, body(): lax.all_gather(ffn_in_latent, 'shard', axis=0, tiled=True)  114 us
    all_gather x1, waiting for transfers between devices, body(): lax.all_gather(teacher_attn, 'shard', axis=1, tiled=True)  92.4 us
    reduce_scatter x1, waiting for transfers between devices, body(): lax.psum_scatter(grad_down.astype(jnp.bfloat16), 'shard', scatter_dimensi...  88 us
    reduce_scatter x1, waiting for transfers between devices, body(): lax.psum_scatter(grad_in.astype(jnp.bfloat16), 'shard', scatter_dimension...  83.9 us
    reduce_scatter x1, waiting for transfers between devices, body(): lax.psum_scatter(value_part.astype(jnp.bfloat16), 'ctx', scatter_dimensio...  47.5 us
    reduce_scatter x1, waiting for transfers between devices, body(): lax.psum_scatter(key_part.astype(jnp.bfloat16), 'ctx', scatter_dimension=...  43 us
  transfers between devices with their start and end apart: 17, of which 13 were waited for; matrix products, arithmetic and copies ran while one was open for 8% of the time, Pallas kernels for 0%

profile of v1, /device:TPU:0, one launch (start us, length us, event | category | flops | bytes accessed | tf_op | source)
XLA Modules:
  0.0 1552.2 jit_solution(4376370647232091068)
XLA Ops:
  9.4 92.4 %all-gather.18.cloned.1.call-done = bf16[4,768,768]{2,1,0:T(8,128)(2,1)} async-done(((bf16[4,192,768]{2,1,0:T(8,128)(2,1)}), bf16[4,768,768]{2,1,0:T(8,128)(2,1)}) %all-gather.18.cloned.1.call-update) | async-done | bytes 4718608 | tf_op jit(solution)/shard_map/all_gather | solution.py:213
  109.9 177.4 %collective-permute-done = f32[768,768]{1,0:T(8,128)} collective-permute-done((f32[768,768]{1,0:T(8,128)S(1)}, f32[768,768]{1,0:T(8,128)}, u32[]{:S(2)}, u32[]{:S(2)}) %collective-permute-start) | collective-permute-done | bytes 2359328 | tf_op jit(solution)/shard_map/ppermute | solution.py:22
  287.3 5.1 maximum_select_fusion.1
  292.4 40.7 %all-gather.10.cloned.1.call-done = f32[4,768,768]{2,1,0:T(8,128)} async-done(((f32[4,192,768]{2,1,0:T(8,128)}), f32[4,768,768]{2,1,0:T(8,128)}) %all-gather.10.cloned.1.call-update) | async-done | bytes 9437200 | tf_op jit(solution)/shard_map/all_gather | solution.py:205
  333.1 4.5 abs_reduce_fusion.2
  339.5 3.1 multiply_convert_fusion.5
  349.1 304.0 %collective-permute-done.1 = f32[1536,768]{1,0:T(8,128)} collective-permute-done((f32[1536,768]{1,0:T(8,128)}, f32[1536,768]{1,0:T(8,128)}, u32[]{:S(2)}, u32[]{:S(2)}) %collective-permute-start.1) | collective-permute-done | bytes 4718624 | tf_op jit(solution)/shard_map/ppermute | solution.py:22
  653.1 7.2 abs_reduce_fusion
  662.1 11.8 multiply_convert_fusion.3
  676.9 16.9 %while.40 = (s32[]{:T(128)}, bf16[2,128,768]{2,1,0:T(8,128)(2,1)S(1)}, bf16[2,1024,768]{1,2,0:T(8,128)(2,1)}, s32[128]{0:T(128)S(1)}, bf16[2,128,768]{2,1,0:T(8,...) while((s32[]{:T(128)}, bf16[2,128,768]{2,1,0:T(8,128)(2,1)S(1)}, ...), condition=%wide.region_22.23_spmd.clone, body=%wide.region_15.0_spmd.clone.sunk | while | flops 414383616 | bytes 37939880 | solution.py:231
  696.0 13.0 fusion.145
  711.2 113.6 %all-gather.16.cloned.1.call-done = f32[768,3072]{1,0:T(8,128)} async-done(((f32[192,3072]{1,0:T(8,128)}), f32[768,3072]{1,0:T(8,128)}) %all-gather.16.cloned.1.call-update) | async-done | bytes 9437200 | tf_op jit(solution)/shard_map/all_gather | solution.py:206
  824.8 4.5 abs_reduce_fusion.1
  829.3 29.0 %all-gather.12.cloned.1.call-done = bf16[2,1024,768]{1,2,0:T(8,128)(2,1)} async-done(((bf16[2,128,768]{1,2,0:T(8,128)(2,1)}), bf16[2,1024,768]{1,2,0:T(8,128)(2,1)}) %all-gather.12.cloned.1.call-update) | async-done | bytes 3145744 | tf_op jit(solution)/shard_map/all_gather | solution.py:223
  858.3 35.3 %all-gather.14.cloned.1.call-done = bf16[2,1024,768]{1,2,0:T(8,128)(2,1)} async-done(((bf16[2,128,768]{1,2,0:T(8,128)(2,1)}), bf16[2,1024,768]{1,2,0:T(8,128)(2,1)}) %all-gather.14.cloned.1.call-update) | async-done | bytes 3145744 | tf_op jit(solution)/shard_map/all_gather | solution.py:222
  893.7 18.2 %while.39 = (s32[]{:T(128)}, bf16[2,128,768]{2,1,0:T(8,128)(2,1)S(1)}, f32[2,12,128]{2,1,0:T(8,128)}, bf16[2,1024,768]{1,2,0:T(8,128)(2,1)}, s32[128]{0:T(128)S(...) while((s32[]{:T(128)}, ...), condition=%wide.region_8.9_spmd.clone, body=%wide.region_1.8_spmd.clone.sunk | while | flops 414386688 | bytes 37561012 | solution.py:241
  914.3 12.7 multiply_convert_fusion.6
  931.7 2.9 fusion.148
  934.6 4.3 multiply_reduce_fusion.4
  942.7 55.9 %while.41 = (s32[]{:T(128)}, f32[2,128,768]{1,2,0:T(8,128)}, bf16[2,1024,768]{2,1,0:T(8,128)(2,1)}, bf16[2,1024,768]{2,1,0:T(8,128)(2,1)}, bf16[2,1024,768]{1,2,...) while((s32[]{:T(128)}, f32[2,128,768]{1,2,0:T(8,128)}, ...), condition=%wide.region_41.42_spmd.clone, body=%wide.region_37.41_spmd.clone.sunk | while | flops 1032224256 | bytes 116177744 | solution.py:273
  1002.1 43.0 %reduce-scatter.5.cloned.1.call-done = bf16[2,128,768]{2,1,0:T(8,128)(2,1)} async-done(((bf16[2,1024,768]{2,1,0:T(8,128)(2,1)}), bf16[2,128,768]{2,1,0:T(8,128)(2,1)}) %reduce-scatter.5.cloned.1.call-update) | async-done | bytes 393232 | tf_op jit(solution)/shard_map/reduce_scatter | solution.py:277
  1047.6 47.5 %reduce-scatter.7.cloned.1.call-done = bf16[2,128,768]{2,1,0:T(8,128)(2,1)} async-done(((bf16[2,1024,768]{2,1,0:T(8,128)(2,1)}), bf16[2,128,768]{2,1,0:T(8,128)(2,1)}) %reduce-scatter.7.cloned.1.call-update) | async-done | bytes 393232 | tf_op jit(solution)/shard_map/reduce_scatter | solution.py:280
  1096.6 3.7 pad_maximum_fusion
  1100.3 8.5 copy.68
  1110.5 4.7 convolution_convert_fusion.1
  1116.8 3.7 convolution_convert_fusion
  1122.4 158.6 %all-reduce.6.cloned.1.call-done = bf16[4,768,768]{2,0,1:T(4,128)(2,1)} async-done(((bf16[4,768,768]{2,0,1:T(4,128)(2,1)}), bf16[4,768,768]{2,0,1:T(4,128)(2,1)}) %all-reduce.6.cloned.1.call-update) | async-done | bytes 4718608
  1283.6 83.9 %reduce-scatter.9.cloned.1.call-done = bf16[192,3072]{1,0:T(8,128)(2,1)} async-done(((bf16[768,3072]{1,0:T(8,128)(2,1)}), bf16[192,3072]{1,0:T(8,128)(2,1)}) %reduce-scatter.9.cloned.1.call-update) | async-done | bytes 1179664 | tf_op jit(solution)/shard_map/reduce_scatter | solution.py:310
  1367.6 88.0 %reduce-scatter.11.cloned.1.call-done = bf16[768,768]{1,0:T(8,128)(2,1)} async-done(((bf16[3072,768]{1,0:T(8,128)(2,1)}), bf16[768,768]{1,0:T(8,128)(2,1)}) %reduce-scatter.11.cloned.1.call-update) | async-done | bytes 1179664 | tf_op jit(solution)/shard_map/reduce_scatter | solution.py:313
  1469.7 41.7 %all-reduce.1 = (f32[4]{0:T(128)S(1)}, f32[12,768]{1,0:T(8,128)S(1)}) all-reduce(f32[4]{0:T(128)S(1)} %pad_maximum_fusion.1, f32[12,768]{1,0:T(8,128)S(1)} %concatenate.41), channel_id=1, replica_groups=mesh['ctx'=8,'shard'=4] {'ctx','shard'}, use_global_device_ids=true, to_apply=%region_31.32 | all-reduce | flops 9220 | bytes 73760 | tf_op jit(solution)/shard_map/psum | solution.py:340
  1518.2 17.2 %all-reduce.8.cloned.1.call-done = (bf16[4,192,768]{2,0,1:T(4,128)(2,1)}, bf16[192,3072]{1,0:T(8,128)(2,1)}, bf16[768,768]{1,0:T(8,128)(2,1)}) async-done(((bf16[4,192,768]{2,0,1:T(4,128)(2,1)}, bf16[192,3072]{1,0:T(8,128)(2,1)}, bf16[768,768]{1,0:T(8,128)(2,1)}), (bf16[4,192,768]{2,0,1:T(4,128)(2,1)}, bf16[192,3072]{1,0:T(8,128)(2,1)}, bf16[768,768]{1,0:T(8,128)(2,1)})) %all-reduce.8.cloned.1.call-update) | async-done | bytes 3538960 | tf_op jit(solution)/shard_map/psum | solution.py:318
  1535.4 3.4 convert_select_fusion.2
  (423 shorter events, 168.3 us)
Async XLA Ops:
  7.2 94.6 %copy-start.12 = (bf16[2,128,768]{2,1,0:T(8,128)(2,1)S(1)}, bf16[2,128,768]{2,1,0:T(8,128)(2,1)}, u32[]{:S(2)}) copy-start(bf16[2,128,768]{2,1,0:T(8,128)(2,1)} %param.18) | copy-start | bytes 1179652
  7.2 94.5 %all-gather.18.cloned.1.call-start = ((), (), s32[]{:S(2)}) async-start(), calls=%async_computation.8 | async-start | bytes 5898240 | tf_op jit(solution)/shard_map/all_gather | solution.py:213
  7.9 325.2 %all-gather.10.cloned.1.call-start = ((), (), s32[]{:S(2)}) async-start(), calls=%async_computation.4 | async-start | bytes 11796480 | tf_op jit(solution)/shard_map/all_gather | solution.py:205
  8.7 668.2 %all-gather.20.cloned.1.call-start = ((), (), s32[]{:S(2)}) async-start(), calls=%async_computation.9 | async-start | bytes 3538944 | tf_op jit(solution)/shard_map/all_gather | solution.py:225
  104.4 572.4 %all-gather.22.cloned.1.call-start = ((), (), s32[]{:S(2)}) async-start(), calls=%async_computation.10 | async-start | bytes 3538944 | tf_op jit(solution)/shard_map/all_gather | solution.py:224
  107.2 588.8 %all-gather.24.cloned.1.call-start = ((), (), s32[]{:S(2)}) async-start(), calls=%async_computation.11 | async-start | bytes 5898240 | tf_op jit(solution)/shard_map/all_gather | solution.py:214
  107.8 588.2 %all-gather.26.cloned.1.call-start = ((), (), s32[]{:S(2)}) async-start(), calls=%async_computation.12 | async-start | bytes 5898240 | tf_op jit(solution)/shard_map/all_gather | solution.py:215
  108.4 716.5 %all-gather.16.cloned.1.call-start = ((), (), s32[]{:S(2)}) async-start(), calls=%async_computation.7 | async-start | bytes 11796480 | tf_op jit(solution)/shard_map/all_gather | solution.py:206
  109.1 749.2 %all-gather.12.cloned.1.call-start = ((), (), s32[]{:S(2)}) async-start(), calls=%async_computation.5 | async-start | bytes 3538944 | tf_op jit(solution)/shard_map/all_gather | solution.py:223
  109.2 178.1 %collective-permute-start = (f32[768,768]{1,0:T(8,128)S(1)}, f32[768,768]{1,0:T(8,128)}, u32[]{:S(2)}, u32[]{:S(2)}) collective-permute-start(f32[768,768]{1,0:T(8,128)S(1)} %copy-done.8), channel_id=1, source_target_pairs={{0,1},{1,0},{2,3},{3,2},{4,5},{5,4},{6,7},{7,6},{8,9},{9,8},{10,11... | collective-permute-start | bytes 7077896 | tf_op jit(solution)/shard_map/ppermute | solution.py:22
  292.4 45.2 %copy-start.52 = (f32[4]{0:T(128)S(1)}, f32[4]{0:T(128)}, u32[]{:S(2)}) copy-start(f32[4]{0:T(128)} %constant.194) | copy-start | bytes 52
  292.4 360.8 %collective-permute-start.1 = (f32[1536,768]{1,0:T(8,128)}, f32[1536,768]{1,0:T(8,128)}, u32[]{:S(2)}, u32[]{:S(2)}) collective-permute-start(f32[1536,768]{1,0:T(8,128)} %maximum_select_fusion.1), channel_id=1, source_target_pairs={{0,2},{1,3},{2,0},{3,1},{4,6},{5,7},{6,4},{7,5},{8,10},{9,11},{10,... | collective-permute-start | bytes 14155784 | tf_op jit(solution)/shard_map/ppermute | solution.py:22
  346.2 547.4 %all-gather.14.cloned.1.call-start = ((), (), s32[]{:S(2)}) async-start(), calls=%async_computation.6 | async-start | bytes 3538944 | tf_op jit(solution)/shard_map/all_gather | solution.py:222
  676.6 368.5 %reduce-scatter.5.cloned.1.call-start = ((), (), s32[]{:S(2)}) async-start(), calls=%async_computation.13 | async-start | bytes 3538944 | tf_op jit(solution)/shard_map/reduce_scatter | solution.py:277
  829.3 84.9 %copy-start.44 = (f32[3072]{0:T(1024)}, f32[3072]{0:T(1024)S(1)}, u32[]{:S(2)}) copy-start(f32[3072]{0:T(1024)S(1)} %broadcast_multiply_fusion) | copy-start | bytes 36868
  893.7 18.3 %copy-start.40 = (f32[768]{0:T(1024)S(1)}, f32[768]{0:T(1024)}, u32[]{:S(2)}) copy-start(f32[768]{0:T(1024)} %get-tuple-element.338) | copy-start | bytes 9220
  911.9 15.1 copy-start.15
  911.9 15.0 slice-start.3
  913.9 25.0 %copy-start.2 = (f32[256,768]{1,0:T(8,128)}, f32[256,768]{1,0:T(8,128)S(1)}, u32[]{:S(2)}) copy-start(f32[256,768]{1,0:T(8,128)S(1)} %get-tuple-element.411) | copy-start | bytes 2359300
  914.2 24.8 %copy-start.42 = (f32[256]{0:T(256)}, f32[256]{0:T(256)S(1)}, u32[]{:S(2)}) copy-start(f32[256]{0:T(256)S(1)} %fusion.84) | copy-start | bytes 3076
  914.2 12.7 slice-start.4
  914.2 12.7 copy-start.51
  998.6 96.4 %reduce-scatter.7.cloned.1.call-start = ((), (), s32[]{:S(2)}) async-start(), calls=%async_computation.14 | async-start | bytes 3538944 | tf_op jit(solution)/shard_map/reduce_scatter | solution.py:280
  999.4 281.6 %all-reduce.6.cloned.1.call-start = ((), (), s32[]{:S(2)}) async-start(), calls=%async_computation.17 | async-start | bytes 9437184
  1108.8 258.7 %reduce-scatter.9.cloned.1.call-start = ((), (), s32[]{:S(2)}) async-start(), calls=%async_computation.15 | async-start | bytes 5898240 | tf_op jit(solution)/shard_map/reduce_scatter | solution.py:310
  1115.2 340.4 %reduce-scatter.11.cloned.1.call-start = ((), (), s32[]{:S(2)}) async-start(), calls=%async_computation.16 | async-start | bytes 5898240 | tf_op jit(solution)/shard_map/reduce_scatter | solution.py:313
  1120.5 414.9 %all-reduce.8.cloned.1.call-start = ((), (), s32[]{:S(2)}) async-start(), calls=%async_computation.18 | async-start | bytes 7077888 | tf_op jit(solution)/shard_map/psum | solution.py:318
  1122.4 333.9 %copy-start.41 = (f32[768]{0:T(1024)S(1)}, f32[768]{0:T(1024)}, u32[]{:S(2)}) copy-start(f32[768]{0:T(1024)} %get-tuple-element.320) | copy-start | bytes 9220
  1283.6 179.8 %copy-start.22 = (f32[2,128,768]{1,2,0:T(8,128)S(1)}, f32[2,128,768]{1,2,0:T(8,128)}, u32[]{:S(2)}) copy-start(f32[2,128,768]{1,2,0:T(8,128)} %get-tuple-element.150) | copy-start | bytes 2359300
  1283.6 182.5 %copy-start.14 = (bf16[2,128,768]{2,1,0:T(8,128)(2,1)S(1)}, bf16[2,128,768]{2,1,0:T(8,128)(2,1)}, u32[]{:S(2)}) copy-start(bf16[2,128,768]{2,1,0:T(8,128)(2,1)} %reduce-scatter.7.cloned.1.call-done) | copy-start | bytes 1179652
  1455.6 57.8 %copy-start.23 = (bf16[2,128,768]{2,1,0:T(8,128)(2,1)S(1)}, bf16[2,128,768]{2,1,0:T(8,128)(2,1)}, u32[]{:S(2)}) copy-start(bf16[2,128,768]{2,1,0:T(8,128)(2,1)} %reduce-scatter.5.cloned.1.call-done) | copy-start | bytes 1179652
  1513.4 22.0 %copy-start.6 = (f32[4,192,768]{2,1,0:T(8,128)S(1)}, f32[4,192,768]{2,1,0:T(8,128)}, u32[]{:S(2)}) copy-start(f32[4,192,768]{2,1,0:T(8,128)} %param.21) | copy-start | bytes 7077892
  (50 other events, 138.8 us)
Sparse Core Ops, SparseCore 0:
  9.6 92.0 all-gather.17
  103.3 229.7 all-gather.9
  335.6 33.8 all-gather.19
  371.8 32.8 all-gather.21
  406.0 127.4 all-gather.23
  535.0 122.0 all-gather.25
  658.6 166.1 all-gather.15
  827.3 30.9 all-gather.11
  860.8 32.8 all-gather.13
  998.8 46.2 reduce-scatter.4
  1048.8 46.2 reduce-scatter.6
  1109.0 171.9 all-reduce.5
  1283.3 84.2 reduce-scatter.8
  1369.7 85.7 reduce-scatter.10
  1459.6 75.7 all-reduce.7
